TPU v7x, 512 devices: a whole 4x4x16 slice. The times are simulated.
512 devices in a mesh: seq: 32 (over x, y, core), exp: 16 (over z).
Axes of the slice: x: 4, y: 4, z: 16, core: 2. Of those that a mesh axis runs over, the one named last changes fastest.
Arguments:
- hidden_in: bfloat16 [16, 4096, 2048], P('exp', 'seq'), may hold values from -6 to 6
- route_ids: int32 [16, 4096, 2], P('exp', 'seq'), may hold values from 0 to 15, all different within a row; in each aligned block of 128 rows (0 to 127, 128 to 255, ..., all dimensions but the last counted through in order) at most 32 rows name the same one
- route_gates: float32 [16, 4096, 2], P('exp', 'seq'), may hold values from 0.1 to 1
- language: int32 [16, 4096], P('exp', 'seq'), may hold values from 0 to 7
- allowed: int32 [8, 8], replicated, may hold values from 0 to 15, all different within a row
- w_gate: bfloat16 [16, 2048, 512], P('exp', 'seq'), may hold values from -0.125 to 0.125
- w_up: bfloat16 [16, 2048, 512], P('exp', 'seq'), may hold values from -0.125 to 0.125
- w_down: bfloat16 [16, 512, 2048], P('exp', 'seq'), may hold values from -0.25 to 0.25
- gate_proj: bfloat16 [2048, 64], replicated, may hold values from -0.125 to 0.125
- head_decay: float32 [32], replicated, may hold values from -13 to -2
- query_in: bfloat16 [16, 4096, 2048], P('exp', 'seq'), may hold values from -6 to 6
- key_in: bfloat16 [16, 4096, 2048], P('exp', 'seq'), may hold values from -6 to 6
- value_in: bfloat16 [16, 4096, 4096], P('exp', 'seq'), may hold values from -6 to 6
- block_inverse: bfloat16 [16, 4096, 2048], P('exp', 'seq'), may hold values from -0.29882812 to 0.29882812
Outputs:
- routed: bfloat16 [16, 4096, 2048], P('exp', 'seq')
- core_out: bfloat16 [16, 4096, 4096], P('exp', 'seq')
Inputs may be any that keep to these rules, and one draw needn't show every extreme that they name: `route_ids`: among the routes of the rows of one device, no expert is named more than 32 times, a bound that some block reaches. `allowed`: each of its rows names 8 different experts, and every expert is allowed for some language.
All inputs are finite; a program needn't handle non-finite values.
Results may differ from a plain program's by a relative error of at most 0.019.
Values may be sent and summed in bfloat16 or wider, within the bound.
A program may use at most 64 MiB of HBM per device.

v0:
```python
import jax
import jax.numpy as jnp
from jax import lax
from jax.sharding import PartitionSpec as P

highest = lax.Precision.HIGHEST


def normalized(values, head_count, factor_scale):
    flat_vals = values.astype(jnp.float32)
    shaped = flat_vals.reshape(flat_vals.shape[0], head_count, -1)
    factor = lax.rsqrt(jnp.sum(shaped * shaped, axis=-1, keepdims=True) + 1e-06) * factor_scale
    return (shaped * factor).astype(jnp.bfloat16)


def delta_blocks(queries, key_rows, values, inverse, beta_gate, decay_log):
    head_count, block_count, block_size, key_dim = queries.shape
    value_dim = values.shape[-1]
    cumulative = jnp.cumsum(decay_log, axis=-1)
    eye_mat = jnp.eye(block_size, dtype=jnp.float32)
    strict = jnp.tril(jnp.ones((block_size, block_size), jnp.float32), -1)
    causal = jnp.tril(jnp.ones((block_size, block_size), jnp.bool_))
    solver = (eye_mat + strict * inverse.astype(jnp.float32)).astype(jnp.bfloat16)
    beta_vals = (beta_gate[..., None] * values.astype(jnp.float32)).astype(jnp.bfloat16)
    beta_keys = (
        (beta_gate * jnp.exp(cumulative))[..., None] * key_rows.astype(jnp.float32)
    ).astype(jnp.bfloat16)
    new_base = jnp.einsum("hnij,hnjd->hnid", solver, beta_vals, preferred_element_type=jnp.float32)
    key_mix = jnp.einsum("hnij,hnjd->hnid", solver, beta_keys, preferred_element_type=jnp.float32)
    query_gate = queries.astype(jnp.float32) * jnp.exp(cumulative)[..., None]
    spread = jnp.where(causal, cumulative[..., :, None] - cumulative[..., None, :], 0.0)
    scores = jnp.einsum("hnid,hnjd->hnij", queries, key_rows, preferred_element_type=jnp.float32)
    weights = jnp.where(causal, scores * jnp.exp(spread), 0.0).astype(jnp.bfloat16)
    tail_decay = jnp.exp(cumulative[..., -1:] - cumulative)
    key_decay = (key_rows.astype(jnp.float32) * tail_decay[..., None]).astype(jnp.bfloat16)
    carry_decay = jnp.exp(cumulative[..., -1])

    def advance(carry_state, inputs):
        mix_now, base_now, gate_now, keyd_now, keep_now = inputs
        fresh_vals = (
            base_now - jnp.einsum("hid,hde->hie", mix_now, carry_state, precision=highest)
        ).astype(jnp.bfloat16)
        early_out = jnp.einsum("hid,hde->hie", gate_now, carry_state, precision=highest)
        carry_state = keep_now[:, None, None] * carry_state + jnp.einsum(
            "hid,hie->hde", keyd_now, fresh_vals, preferred_element_type=jnp.float32
        )
        return (carry_state, (fresh_vals, early_out))

    moved_seq = tuple(
        (
            jnp.moveaxis(element, 1, 0)
            for element in (key_mix, new_base, query_gate, key_decay, carry_decay)
        )
    )
    initial = jnp.zeros((head_count, key_dim, value_dim), jnp.float32)
    _, (fresh_vals, early_out) = lax.scan(advance, initial, moved_seq)
    fresh_vals = jnp.moveaxis(fresh_vals, 0, 1)
    early_out = jnp.moveaxis(early_out, 0, 1)
    local_out = jnp.einsum(
        "hnij,hnjd->hnid", weights, fresh_vals, preferred_element_type=jnp.float32
    )
    return (early_out + local_out).astype(jnp.bfloat16)


def per_device(
    hidden_in,
    route_ids,
    route_gates,
    language,
    allowed,
    w_gate,
    w_up,
    w_down,
    gate_proj,
    head_decay,
    query_in,
    key_in,
    value_in,
    block_inverse,
):
    exp_size = lax.axis_size("exp")
    seq_size = lax.axis_size("seq")
    tokens = hidden_in[0]
    tok_rows, model_width = tokens.shape
    routes_tok = route_ids.shape[2]
    experts = exp_size * w_gate.shape[0]
    capacity = 2 * tok_rows * routes_tok // experts
    flat_routes = route_ids[0].reshape(-1)
    expert_range = jnp.arange(experts, dtype=jnp.int32)
    onehot = (flat_routes[:, None] == expert_range[None, :]).astype(jnp.int32)
    earlier = jnp.cumsum(onehot, axis=0) - onehot
    slot_index = jnp.sum(earlier * onehot, axis=1)
    target = flat_routes * capacity + slot_index
    route_token = jnp.arange(tok_rows * routes_tok, dtype=jnp.int32) // routes_tok
    source_row = jnp.full((experts * capacity,), tok_rows, jnp.int32).at[target].set(route_token)
    padded = jnp.concatenate([tokens, jnp.zeros((1, model_width), tokens.dtype)], axis=0)
    outgoing = jnp.take(padded, source_row, axis=0).reshape(experts, capacity, model_width)
    incoming = lax.all_to_all(outgoing, "exp", split_axis=0, concat_axis=0, tiled=True)
    expert_rows = incoming.reshape(-1, model_width)

    def add_rows(portion):
        return jnp.dot(expert_rows, portion, preferred_element_type=jnp.float32)

    gate_proj_h = add_rows(lax.all_gather(w_gate[0], "seq", axis=0, tiled=True))
    up_proj_h = add_rows(lax.all_gather(w_up[0], "seq", axis=0, tiled=True))
    hidden = (jax.nn.silu(gate_proj_h) * up_proj_h).astype(jnp.bfloat16)
    produced = jnp.dot(
        hidden,
        lax.all_gather(w_down[0], "seq", axis=0, tiled=True),
        preferred_element_type=jnp.float32,
    )
    produced = produced.astype(jnp.bfloat16).reshape(exp_size, -1, model_width)
    returned = lax.all_to_all(produced, "exp", split_axis=0, concat_axis=0, tiled=True)
    back_rows = jnp.take(returned.reshape(-1, model_width), target, axis=0).reshape(
        tok_rows, routes_tok, model_width
    )
    lang_count = allowed.shape[0]
    lang_table = jnp.any(allowed[:, :, None] == expert_range[None, None, :], axis=1).astype(
        jnp.float32
    )
    lang_hot = (language[0][:, None] == jnp.arange(lang_count, dtype=jnp.int32)[None, :]).astype(
        jnp.float32
    )
    token_allow = jnp.dot(lang_hot, lang_table, precision=highest)
    route_allow = jnp.sum(
        token_allow[:, None, :] * onehot.reshape(tok_rows, routes_tok, experts).astype(jnp.float32),
        axis=2,
    )
    route_weight = route_gates[0] * route_allow
    mixed = jnp.sum(route_weight[..., None] * back_rows.astype(jnp.float32), axis=1)
    routed = mixed.astype(jnp.bfloat16)
    residual = (tokens.astype(jnp.float32) + routed.astype(jnp.float32)).astype(jnp.bfloat16)
    logits = jnp.dot(residual, gate_proj, preferred_element_type=jnp.float32).astype(jnp.bfloat16)
    heads_v = head_decay.shape[0]
    heads_k = heads_v // 2
    key_dim = query_in.shape[2] // heads_k
    heads_dev = heads_v // seq_size
    beta_logit = logits[:, :heads_v]
    decay_logit = logits[:, heads_v:]
    queries = query_in[0]
    key_rows = key_in[0]
    values_in = value_in[0]
    inverse_in = block_inverse[0]

    def repeated(values):
        return jnp.repeat(values.reshape(tok_rows, heads_k, key_dim), 2, axis=1).reshape(
            tok_rows, -1
        )

    full_q, full_k, got_v, got_inv, got_beta, got_decay = (
        lax.all_to_all(repeated(queries), "seq", split_axis=1, concat_axis=0, tiled=True),
        lax.all_to_all(repeated(key_rows), "seq", split_axis=1, concat_axis=0, tiled=True),
        lax.all_to_all(values_in, "seq", split_axis=1, concat_axis=0, tiled=True),
        lax.all_to_all(inverse_in, "seq", split_axis=1, concat_axis=0, tiled=True),
        lax.all_to_all(beta_logit, "seq", split_axis=1, concat_axis=0, tiled=True),
        lax.all_to_all(decay_logit, "seq", split_axis=1, concat_axis=0, tiled=True),
    )
    seq_len = full_q.shape[0]
    block_size = inverse_in.shape[1] // heads_v
    block_count = seq_len // block_size
    query_n = normalized(full_q, heads_dev, key_dim ** (-0.5))
    key_n = normalized(full_k, heads_dev, 0.5)

    def arrange(values):
        return values.reshape(block_count, block_size, heads_dev, -1).transpose(2, 0, 1, 3)

    head_start = lax.axis_index("seq") * heads_dev
    decay_rate = jnp.exp(lax.dynamic_slice_in_dim(head_decay, head_start, heads_dev))
    beta_gate = jax.nn.sigmoid(got_beta.astype(jnp.float32))
    decay_log = -decay_rate[None, :] * jax.nn.softplus(got_decay.astype(jnp.float32))
    result = delta_blocks(
        arrange(query_n),
        arrange(key_n),
        arrange(got_v.reshape(seq_len, heads_dev, -1)),
        arrange(got_inv.reshape(seq_len, heads_dev, block_size)),
        beta_gate.reshape(block_count, block_size, heads_dev).transpose(2, 0, 1),
        decay_log.reshape(block_count, block_size, heads_dev).transpose(2, 0, 1),
    )
    flat_out = result.transpose(1, 2, 0, 3).reshape(seq_len, -1)
    core_out = lax.all_to_all(flat_out, "seq", split_axis=0, concat_axis=1, tiled=True)
    return (routed[None], core_out[None])


def solution(mesh):
    in_specs = (
        P("exp", "seq", None),
        P("exp", "seq", None),
        P("exp", "seq", None),
        P("exp", "seq"),
        P(),
        P("exp", "seq", None),
        P("exp", "seq", None),
        P("exp", "seq", None),
        P(),
        P(),
        P("exp", "seq", None),
        P("exp", "seq", None),
        P("exp", "seq", None),
        P("exp", "seq", None),
    )
    out_specs = (P("exp", "seq", None), P("exp", "seq", None))
    return jax.shard_map(
        per_device, mesh=mesh, in_specs=in_specs, out_specs=out_specs, check_vma=False
    )
```

profile of v0, /device:TPU:33, one launch (start us, length us, event | category | flops | bytes accessed | tf_op | source)
XLA Modules:
  0.0 757.4 jit_solution(230179408285907515)
XLA Ops:
  10.0 7.8 %all-to-all-start.4 = ((bf16[128,32,64]{0,2,1:T(8,128)(2,1)}), bf16[128,32,64]{0,2,1:T(8,128)(2,1)S(1)}, u32[]{:S(2)}, u32[]{:S(2)}) async-start(bf16[128,32,64]{0,2,1:T(8,128)(2,1)} %bitcast.23), calls=%async_computation.4 | async-start | bytes 1048576 | tf_op jit(solution)/shard_map/all_to_all | solution.py:154
  21.0 8.3 %all-to-all-done.4 = bf16[128,32,64]{0,2,1:T(8,128)(2,1)S(1)} async-done(((bf16[128,32,64]{0,2,1:T(8,128)(2,1)}), bf16[128,32,64]{0,2,1:T(8,128)(2,1)S(1)}, u32[]{:S(2)}, u32[]{:S(2)}) %all-to-all-start.4) | async-done | bytes 524320 | tf_op jit(solution)/shard_map/all_to_all | solution.py:154
  30.6 3.7 all-to-all-start.3
  34.5 3.3 gather_fusion
  41.0 10.8 %all-to-all-done.3 = bf16[128,32,128]{2,0,1:T(8,128)(2,1)S(1)} async-done(((bf16[128,32,128]{2,0,1:T(8,128)(2,1)}), bf16[128,32,128]{2,0,1:T(8,128)(2,1)S(1)}, u32[]{:S(2)}, u32[]{:S(2)}) %all-to-all-start.3) | async-done | bytes 1048608 | tf_op jit(solution)/shard_map/all_to_all | solution.py:152
  51.8 14.3 %all-to-all-start = ((bf16[16,32,2048]{2,1,0:T(8,128)(2,1)}), bf16[16,32,2048]{2,1,0:T(8,128)(2,1)}, u32[]{:S(2)}, u32[]{:S(2)}) async-start(bf16[16,32,2048]{2,1,0:T(8,128)(2,1)} %broadcast_select_fusion), calls=%async_computation | async-start | bytes 4194304 | tf_op jit(solution)/shard_map/all_to_all | solution.py:98
  67.9 90.8 %all-to-all-done = bf16[16,32,2048]{2,1,0:T(8,128)(2,1)} async-done(((bf16[16,32,2048]{2,1,0:T(8,128)(2,1)}), bf16[16,32,2048]{2,1,0:T(8,128)(2,1)}, u32[]{:S(2)}, u32[]{:S(2)}) %all-to-all-start) | async-done | bytes 2097184 | tf_op jit(solution)/shard_map/all_to_all | solution.py:98
  159.9 6.3 all-to-all-start.7
  166.3 3.5 fusion.26
  169.8 40.0 %all-gather.9.cloned.1.call-done = bf16[1,2048,512]{2,1,0:T(8,128)(2,1)} async-done(((bf16[1,64,512]{2,1,0:T(8,128)(2,1)}), bf16[1,2048,512]{2,1,0:T(8,128)(2,1)}) %all-gather.9.cloned.1.call-update) | async-done | bytes 2097168 | tf_op jit(solution)/shard_map/all_gather | solution.py:105
  209.8 6.7 convolution_convert_fusion
  217.4 12.1 %all-to-all-start.1 = ((bf16[16,32,2048]{2,1,0:T(8,128)(2,1)}), bf16[16,32,2048]{2,1,0:T(8,128)(2,1)S(1)}, u32[]{:S(2)}, u32[]{:S(2)}) async-start(bf16[16,32,2048]{2,1,0:T(8,128)(2,1)} %bitcast.187), calls=%async_computation.1 | async-start | bytes 4194304 | tf_op jit(solution)/shard_map/all_to_all | solution.py:113
  256.5 65.6 %all-to-all-done.1 = bf16[16,32,2048]{2,1,0:T(8,128)(2,1)S(1)} async-done(((bf16[16,32,2048]{2,1,0:T(8,128)(2,1)}), bf16[16,32,2048]{2,1,0:T(8,128)(2,1)S(1)}, u32[]{:S(2)}, u32[]{:S(2)}) %all-to-all-start.1) | async-done | bytes 2097184 | tf_op jit(solution)/shard_map/all_to_all | solution.py:113
  322.1 7.7 %all-to-all-start.6 = ((bf16[128,32,128]{2,0,1:T(8,128)(2,1)}), bf16[128,32,128]{2,0,1:T(8,128)(2,1)}, u32[]{:S(2)}, u32[]{:S(2)}) async-start(bf16[128,32,128]{2,0,1:T(8,128)(2,1)} %copy.130), calls=%async_computation.6 | async-start | bytes 2097152 | tf_op jit(solution)/shard_map/all_to_all | solution.py:153
  336.5 4.1 multiply_reduce_fusion.2
  342.4 4.4 all-to-all-done.6
  346.8 4.0 all-to-all-start.2
  358.1 7.4 all-to-all-start.5
  368.1 4.5 all-to-all-done.5
  374.8 3.7 convolution_bitcast_fusion.3
  381.0 3.7 convert_multiply_fusion
  384.7 339.8 %while.15 = (s32[]{:T(128)}, f32[1,128,128]{2,1,0:T(8,128)S(1)}, bf16[64,1,64,128]{3,2,1,0:T(8,128)(2,1)}, f32[64,1,64,128]{3,2,1,0:T(8,128)}, f32[64,1]{0,1:T(1...) while((s32[]{:T(128)}, f32[1,128,128]{2,1,0:T(8,128)S(1)}, ...), condition=%wide.region_11.12_spmd.clone, body=%wide.region_10.11_spmd.clone.sunk | while | flops 27361284 | bytes 461957 | solution.py:56
  724.5 3.9 fusion.22
  728.3 20.6 %all_to_all.104 = bf16[32,128,128]{2,1,0:T(8,128)(2,1)S(1)} all-to-all(bf16[32,128,128]{2,1,0:T(8,128)(2,1)S(1)} %bitcast.184), channel_id=1, replica_groups=mesh['seq'=32,'exp'=16] {'seq'}, dimensions={0} | all-to-all | bytes 2097152 | tf_op jit(solution)/shard_map/all_to_all | solution.py:180
  (381 shorter events, 404.1 us)
Async XLA Ops:
  7.2 334.3 %copy-start = (bf16[2048,64]{0,1:T(8,128)(2,1)S(1)}, bf16[2048,64]{0,1:T(8,128)(2,1)}, u32[]{:S(2)}) copy-start(bf16[2048,64]{0,1:T(8,128)(2,1)} %param.24) | copy-start | bytes 786436
  7.2 10.6 %copy-start.15 = (s32[1,128,2]{1,2,0:T(2,128)S(1)}, s32[1,128,2]{1,2,0:T(2,128)}, u32[]{:S(2)}) copy-start(s32[1,128,2]{1,2,0:T(2,128)} %param.17) | copy-start | bytes 3076
  7.2 12.1 %copy-start.8 = (bf16[1,128,2048]{2,1,0:T(8,128)(2,1)S(1)}, bf16[1,128,2048]{2,1,0:T(8,128)(2,1)}, u32[]{:S(2)}) copy-start(bf16[1,128,2048]{2,1,0:T(8,128)(2,1)} %param.27) | copy-start | bytes 1572868
  7.2 159.1 %all-gather.7.cloned.1.call-start = ((), (), s32[]{:S(2)}) async-start(), calls=%async_computation.9 | async-start | bytes 2162688 | tf_op jit(solution)/shard_map/all_gather | solution.py:104
  10.0 19.4 %all-to-all-start.4 = ((bf16[128,32,64]{0,2,1:T(8,128)(2,1)}), bf16[128,32,64]{0,2,1:T(8,128)(2,1)S(1)}, u32[]{:S(2)}, u32[]{:S(2)}) async-start(bf16[128,32,64]{0,2,1:T(8,128)(2,1)} %bitcast.23), calls=%async_computation.4 | async-start | bytes 1048576 | tf_op jit(solution)/shard_map/all_to_all | solution.py:154
  19.5 14.9 %copy-start.6 = (bf16[1,128,2048]{2,1,0:T(8,128)(2,1)S(1)}, bf16[1,128,2048]{2,1,0:T(8,128)(2,1)}, u32[]{:S(2)}) copy-start(bf16[1,128,2048]{2,1,0:T(8,128)(2,1)} %param.16) | copy-start | bytes 1572868
  19.6 10.9 %copy-start.16 = (s32[256,1]{0,1:T(1,128)}, s32[256,1]{0,1:T(1,128)S(1)}, u32[]{:S(2)}) copy-start(s32[256,1]{0,1:T(1,128)S(1)} %compare_select_fusion.1) | copy-start | bytes 3076
  30.6 21.3 %all-to-all-start.3 = ((bf16[128,32,128]{2,0,1:T(8,128)(2,1)}), bf16[128,32,128]{2,0,1:T(8,128)(2,1)S(1)}, u32[]{:S(2)}, u32[]{:S(2)}) async-start(bf16[128,32,128]{2,0,1:T(8,128)(2,1)} %bitcast.18), calls=%async_computation.3 | async-start | bytes 2097152 | tf_op jit(solution)/shard_map/all_to_all | solution.py:152
  41.0 26.7 %copy-start.9 = (bf16[1,128,2048]{2,1,0:T(8,128)(2,1)S(1)}, bf16[1,128,2048]{2,1,0:T(8,128)(2,1)}, u32[]{:S(2)}) copy-start(bf16[1,128,2048]{2,1,0:T(8,128)(2,1)} %param.26) | copy-start | bytes 1572868
  51.8 106.9 %all-to-all-start = ((bf16[16,32,2048]{2,1,0:T(8,128)(2,1)}), bf16[16,32,2048]{2,1,0:T(8,128)(2,1)}, u32[]{:S(2)}, u32[]{:S(2)}) async-start(bf16[16,32,2048]{2,1,0:T(8,128)(2,1)} %broadcast_select_fusion), calls=%async_computation | async-start | bytes 4194304 | tf_op jit(solution)/shard_map/all_to_all | solution.py:98
  66.2 103.6 %all-gather.11.cloned.1.call-start = ((), (), s32[]{:S(2)}) async-start(), calls=%async_computation.11 | async-start | bytes 2162688 | tf_op jit(solution)/shard_map/all_gather | solution.py:109
  66.9 142.9 %all-gather.9.cloned.1.call-start = ((), (), s32[]{:S(2)}) async-start(), calls=%async_computation.10 | async-start | bytes 2162688 | tf_op jit(solution)/shard_map/all_gather | solution.py:105
  159.9 56.5 %all-to-all-start.7 = ((bf16[128,32,128]{2,0,1:T(8,128)(2,1)}), bf16[128,32,128]{2,0,1:T(8,128)(2,1)S(1)}, u32[]{:S(2)}, u32[]{:S(2)}) async-start(bf16[128,32,128]{2,0,1:T(8,128)(2,1)} %bitcast.35), calls=%async_computation.7 | async-start | bytes 2097152 | tf_op jit(solution)/shard_map/all_to_all | solution.py:151
  217.4 104.7 %all-to-all-start.1 = ((bf16[16,32,2048]{2,1,0:T(8,128)(2,1)}), bf16[16,32,2048]{2,1,0:T(8,128)(2,1)S(1)}, u32[]{:S(2)}, u32[]{:S(2)}) async-start(bf16[16,32,2048]{2,1,0:T(8,128)(2,1)} %bitcast.187), calls=%async_computation.1 | async-start | bytes 4194304 | tf_op jit(solution)/shard_map/all_to_all | solution.py:113
  322.1 24.6 %all-to-all-start.6 = ((bf16[128,32,128]{2,0,1:T(8,128)(2,1)}), bf16[128,32,128]{2,0,1:T(8,128)(2,1)}, u32[]{:S(2)}, u32[]{:S(2)}) async-start(bf16[128,32,128]{2,0,1:T(8,128)(2,1)} %copy.130), calls=%async_computation.6 | async-start | bytes 2097152 | tf_op jit(solution)/shard_map/all_to_all | solution.py:153
  334.7 6.7 copy-start.7
  334.7 16.0 %copy-start.12 = (f32[128,32]{0,1:T(8,128)S(1)}, f32[128,32]{0,1:T(8,128)}, u32[]{:S(2)}) copy-start(f32[128,32]{0,1:T(8,128)} %multiply_reduce_fusion) | copy-start | bytes 49156
  334.7 16.0 %copy-start.13 = (f32[32,128]{1,0:T(8,128)S(1)}, f32[32,128]{1,0:T(8,128)}, u32[]{:S(2)}) copy-start(f32[32,128]{1,0:T(8,128)} %multiply_bitcast_fusion.1) | copy-start | bytes 49156
  346.8 11.3 %all-to-all-start.2 = ((bf16[128,32,1]{0,2,1:T(2,128)(2,1)}), bf16[128,32,1]{0,2,1:T(2,128)(2,1)S(1)}, u32[]{:S(2)}, u32[]{:S(2)}) async-start(bf16[128,32,1]{0,2,1:T(2,128)(2,1)} %copy.123), calls=%async_computation.2 | async-start | bytes 32768 | tf_op jit(solution)/shard_map/all_to_all | solution.py:156
  354.6 20.2 %copy-start.3 = (bf16[64,64,64]{2,1,0:T(8,128)(2,1)S(1)}, bf16[64,64,64]{2,1,0:T(8,128)(2,1)}, u32[]{:S(2)}) copy-start(bf16[64,64,64]{2,1,0:T(8,128)(2,1)} %copy.131) | copy-start | bytes 1572868
  358.1 14.4 %all-to-all-start.5 = ((bf16[128,32,1]{0,2,1:T(2,128)(2,1)}), bf16[128,32,1]{0,2,1:T(2,128)(2,1)}, u32[]{:S(2)}, u32[]{:S(2)}) async-start(bf16[128,32,1]{0,2,1:T(2,128)(2,1)} %copy.127), calls=%async_computation.5 | async-start | bytes 32768 | tf_op jit(solution)/shard_map/all_to_all | solution.py:155
  381.0 3.7 copy-start.17
  384.7 339.8 %copy-start.11 = (f32[64,64]{1,0:T(8,128)S(1)}, f32[64,64]{1,0:T(8,128)}, u32[]{:S(2)}) copy-start(f32[64,64]{1,0:T(8,128)} %mul.296) | copy-start | bytes 49156
  384.7 339.8 %copy-start.14 = (pred[64,64]{1,0:T(8,128)(4,1)S(1)}, pred[64,64]{1,0:T(8,128)(4,1)}, u32[]{:S(2)}) copy-start(pred[64,64]{1,0:T(8,128)(4,1)} %iota_compare_fusion.2) | copy-start | bytes 12292
  (5 other events, 8.0 us)
Sparse Core Ops, SparseCore 0:
  11.2 70.7 all-gather.6
  85.1 58.4 all-gather.10
  146.7 63.0 all-gather.8
where the time goes:
time: 772 us; the launch traced here: 757 us
  matrix products  319 us (41%)
  waiting for transfers between devices  227 us (29%)
  local copies, waits for them, and re-layouts  77.4 us (10%)
  starting transfers between devices  63.4 us (8%)
  other arithmetic  34.6 us (4%)
  blocking collectives  20.6 us (3%)
  between operations  14.9 us (2%)
    dot_general x64, matrix products, advance(): jnp.einsum('hid,hde->hie', mix_now, carry_state, precision=highest)  100 us
    dot_general x64, matrix products, advance(): jnp.einsum('hid,hde->hie', gate_now, carry_state, precision=highest)  99.6 us
    dot_general x64, matrix products, advance(): jnp.einsum('hid,hie->hde', keyd_now, fresh_vals, preferred_element_type=j...  97.4 us
    all_to_all x1, waiting for transfers between devices, per_device(): lax.all_to_all(outgoing, 'exp', split_axis=0, concat_axis=0, tiled=True)  90.8 us
    all_to_all x1, waiting for transfers between devices, per_device(): lax.all_to_all(produced, 'exp', split_axis=0, concat_axis=0, tiled=True)  65.6 us
    dynamic_slice x64, local copies, waits for them, and re-layouts, delta_blocks(): _, (fresh_vals, early_out) = lax.scan(advance, initial, moved_seq)  41.1 us
    all_gather x1, waiting for transfers between devices, per_device(): up_proj_h = add_rows(lax.all_gather(w_up[0], 'seq', axis=0, tiled=True))  40 us
    all_to_all x1, blocking collectives, per_device(): lax.all_to_all(flat_out, 'seq', split_axis=0, concat_axis=1, tiled=True)  20.6 us
  transfers between devices with their start and end apart: 11, of which 7 were waited for; matrix products, arithmetic and copies ran while one was open for 10% of the time, Pallas kernels for 0%

commit v1 on v0

--- a/solution.py
+++ b/solution.py
@@ -4,6 +4,12 @@
 from jax.sharding import PartitionSpec as P
 
 highest = lax.Precision.HIGHEST
+
+
+def stacked_exchange(x, mesh_axis, split, join):
+    pieces = jnp.split(x, lax.axis_size(mesh_axis), axis=split)
+    received = lax.all_to_all(jnp.stack(pieces), mesh_axis, 0, 0)
+    return jnp.concatenate(received, axis=join)
 
 
 def normalized(values, head_count, factor_scale):
@@ -151,7 +157,7 @@
         lax.all_to_all(repeated(queries), "seq", split_axis=1, concat_axis=0, tiled=True),
         lax.all_to_all(repeated(key_rows), "seq", split_axis=1, concat_axis=0, tiled=True),
         lax.all_to_all(values_in, "seq", split_axis=1, concat_axis=0, tiled=True),
-        lax.all_to_all(inverse_in, "seq", split_axis=1, concat_axis=0, tiled=True),
+        stacked_exchange(inverse_in, "seq", 1, 0),
         lax.all_to_all(beta_logit, "seq", split_axis=1, concat_axis=0, tiled=True),
         lax.all_to_all(decay_logit, "seq", split_axis=1, concat_axis=0, tiled=True),
     )

time: 772 us -> 772 us (level)
  local copies, waits for them, and re-layouts: 77.4 us -> 96.8 us
  waiting for transfers between devices: 227 us -> 212 us
    unnamed x41 -> x72, local copies, waits for them, and re-layouts: 6.49 us -> 24.6 us
    all_gather x1, waiting for transfers between devices: 40 us -> 22.5 us  [per_device(): up_proj_h = add_rows(lax.all_gather(w_up[0], 'seq', axis=0, tiled=True))]
  transfers between devices with their start and end apart: 11 -> 11, of which waited for: 7 -> 7; matrix products, arithmetic and copies ran while one was open for 10% -> 12% of each run, Pallas kernels for 0% -> 0%
where the time goes in v1:
time: 772 us; the launch traced here: 758 us
  matrix products  319 us (41%)
  waiting for transfers between devices  212 us (27%)
  local copies, waits for them, and re-layouts  96.8 us (13%)
  starting transfers between devices  60.5 us (8%)
  other arithmetic  33.5 us (4%)
  blocking collectives  20.6 us (3%)
  between operations  14.9 us (2%)
    dot_general x64, matrix products, advance(): jnp.einsum('hid,hde->hie', mix_now, carry_state, precision=highest)  100 us
    dot_general x64, matrix products, advance(): jnp.einsum('hid,hde->hie', gate_now, carry_state, precision=highest)  99.6 us
    dot_general x64, matrix products, advance(): jnp.einsum('hid,hie->hde', keyd_now, fresh_vals, preferred_element_type=j...  97.4 us
    all_to_all x1, waiting for transfers between devices, per_device(): lax.all_to_all(outgoing, 'exp', split_axis=0, concat_axis=0, tiled=True)  91.9 us
    all_to_all x1, waiting for transfers between devices, per_device(): lax.all_to_all(produced, 'exp', split_axis=0, concat_axis=0, tiled=True)  66.1 us
    dynamic_slice x64, local copies, waits for them, and re-layouts, delta_blocks(): _, (fresh_vals, early_out) = lax.scan(advance, initial, moved_seq)  41.1 us
    unnamed x72, local copies, waits for them, and re-layouts  24.6 us
    all_gather x1, waiting for transfers between devices, per_device(): up_proj_h = add_rows(lax.all_gather(w_up[0], 'seq', axis=0, tiled=True))  22.5 us
  transfers between devices with their start and end apart: 11, of which 7 were waited for; matrix products, arithmetic and copies ran while one was open for 12% of the time, Pallas kernels for 0%

profile of v1, /device:TPU:33, one launch (start us, length us, event | category | flops | bytes accessed | tf_op | source)
XLA Modules:
  0.0 757.8 jit_solution(14139185713661344212)
XLA Ops:
  28.7 7.8 %all-to-all-start.4 = ((bf16[32,128,64]{1,2,0:T(8,128)(2,1)}), bf16[32,128,64]{1,2,0:T(8,128)(2,1)S(1)}, u32[]{:S(2)}, u32[]{:S(2)}) async-start(bf16[32,128,64]{1,2,0:T(8,128)(2,1)} %constant_dynamic-update-slice_fusion), calls=%async_computation.4 | async-start | bytes 1048576 | tf_op jit(solution)/shard_map/all_to_all | solution.py:11
  39.7 8.8 %all-to-all-done.4 = bf16[32,128,64]{1,2,0:T(8,128)(2,1)S(1)} async-done(((bf16[32,128,64]{1,2,0:T(8,128)(2,1)}), bf16[32,128,64]{1,2,0:T(8,128)(2,1)S(1)}, u32[]{:S(2)}, u32[]{:S(2)}) %all-to-all-start.4) | async-done | bytes 524320 | tf_op jit(solution)/shard_map/all_to_all | solution.py:11
  49.7 3.7 all-to-all-start.3
  53.6 3.3 gather_fusion
  60.1 11.4 %all-to-all-done.3 = bf16[128,32,128]{2,0,1:T(8,128)(2,1)S(1)} async-done(((bf16[128,32,128]{2,0,1:T(8,128)(2,1)}), bf16[128,32,128]{2,0,1:T(8,128)(2,1)S(1)}, u32[]{:S(2)}, u32[]{:S(2)}) %all-to-all-start.3) | async-done | bytes 1048608 | tf_op jit(solution)/shard_map/all_to_all | solution.py:158
  71.5 15.4 %all-to-all-start = ((bf16[16,32,2048]{2,1,0:T(8,128)(2,1)}), bf16[16,32,2048]{2,1,0:T(8,128)(2,1)}, u32[]{:S(2)}, u32[]{:S(2)}) async-start(bf16[16,32,2048]{2,1,0:T(8,128)(2,1)} %broadcast_select_fusion), calls=%async_computation | async-start | bytes 4194304 | tf_op jit(solution)/shard_map/all_to_all | solution.py:104
  88.7 91.9 %all-to-all-done = bf16[16,32,2048]{2,1,0:T(8,128)(2,1)} async-done(((bf16[16,32,2048]{2,1,0:T(8,128)(2,1)}), bf16[16,32,2048]{2,1,0:T(8,128)(2,1)}, u32[]{:S(2)}, u32[]{:S(2)}) %all-to-all-start) | async-done | bytes 2097184 | tf_op jit(solution)/shard_map/all_to_all | solution.py:104
  181.8 5.0 all-to-all-start.7
  186.8 3.5 fusion.26
  190.3 22.5 %all-gather.9.cloned.1.call-done = bf16[1,2048,512]{2,1,0:T(8,128)(2,1)} async-done(((bf16[1,64,512]{2,1,0:T(8,128)(2,1)}), bf16[1,2048,512]{2,1,0:T(8,128)(2,1)}) %all-gather.9.cloned.1.call-update) | async-done | bytes 2097168 | tf_op jit(solution)/shard_map/all_gather | solution.py:111
  212.8 6.6 convolution_convert_fusion
  220.5 9.9 %all-to-all-start.1 = ((bf16[16,32,2048]{2,1,0:T(8,128)(2,1)}), bf16[16,32,2048]{2,1,0:T(8,128)(2,1)S(1)}, u32[]{:S(2)}, u32[]{:S(2)}) async-start(bf16[16,32,2048]{2,1,0:T(8,128)(2,1)} %bitcast.345), calls=%async_computation.1 | async-start | bytes 4194304 | tf_op jit(solution)/shard_map/all_to_all | solution.py:119
  256.9 66.1 %all-to-all-done.1 = bf16[16,32,2048]{2,1,0:T(8,128)(2,1)S(1)} async-done(((bf16[16,32,2048]{2,1,0:T(8,128)(2,1)}), bf16[16,32,2048]{2,1,0:T(8,128)(2,1)S(1)}, u32[]{:S(2)}, u32[]{:S(2)}) %all-to-all-start.1) | async-done | bytes 2097184 | tf_op jit(solution)/shard_map/all_to_all | solution.py:119
  322.9 7.2 all-to-all-start.6
  336.9 4.1 multiply_reduce_fusion.2
  342.8 4.4 all-to-all-done.6
  347.1 4.0 all-to-all-start.2
  358.5 7.4 all-to-all-start.5
  368.5 4.5 all-to-all-done.5
  375.2 3.7 convolution_bitcast_fusion.3
  381.4 3.7 convert_multiply_fusion
  385.1 339.7 %while.15 = (s32[]{:T(128)}, f32[1,128,128]{2,1,0:T(8,128)S(1)}, bf16[64,1,64,128]{3,2,1,0:T(8,128)(2,1)}, f32[64,1,64,128]{3,2,1,0:T(8,128)}, f32[64,1]{0,1:T(1...) while((s32[]{:T(128)}, f32[1,128,128]{2,1,0:T(8,128)S(1)}, ...), condition=%wide.region_11.12_spmd.clone, body=%wide.region_10.11_spmd.clone.sunk | while | flops 27361284 | bytes 461957 | solution.py:62
  724.9 3.9 fusion.22
  728.7 20.6 %all_to_all.96 = bf16[32,128,128]{2,1,0:T(8,128)(2,1)S(1)} all-to-all(bf16[32,128,128]{2,1,0:T(8,128)(2,1)S(1)} %bitcast.310), channel_id=1, replica_groups=mesh['seq'=32,'exp'=16] {'seq'}, dimensions={0} | all-to-all | bytes 2097152 | tf_op jit(solution)/shard_map/all_to_all | solution.py:186
  (412 shorter events, 422.4 us)
Async XLA Ops:
  7.2 334.7 %copy-start = (bf16[2048,64]{0,1:T(8,128)(2,1)S(1)}, bf16[2048,64]{0,1:T(8,128)(2,1)}, u32[]{:S(2)}) copy-start(bf16[2048,64]{0,1:T(8,128)(2,1)} %param.24) | copy-start | bytes 786436
  7.2 29.3 %copy-start.15 = (s32[1,128,2]{1,2,0:T(2,128)S(1)}, s32[1,128,2]{1,2,0:T(2,128)}, u32[]{:S(2)}) copy-start(s32[1,128,2]{1,2,0:T(2,128)} %param.17) | copy-start | bytes 3076
  7.2 30.8 %copy-start.8 = (bf16[1,128,2048]{2,1,0:T(8,128)(2,1)S(1)}, bf16[1,128,2048]{2,1,0:T(8,128)(2,1)}, u32[]{:S(2)}) copy-start(bf16[1,128,2048]{2,1,0:T(8,128)(2,1)} %param.27) | copy-start | bytes 1572868
  7.2 179.6 %all-gather.7.cloned.1.call-start = ((), (), s32[]{:S(2)}) async-start(), calls=%async_computation.9 | async-start | bytes 2162688 | tf_op jit(solution)/shard_map/all_gather | solution.py:110
  28.7 19.8 %all-to-all-start.4 = ((bf16[32,128,64]{1,2,0:T(8,128)(2,1)}), bf16[32,128,64]{1,2,0:T(8,128)(2,1)S(1)}, u32[]{:S(2)}, u32[]{:S(2)}) async-start(bf16[32,128,64]{1,2,0:T(8,128)(2,1)} %constant_dynamic-update-slice_fusion), calls=%async_computation.4 | async-start | bytes 1048576 | tf_op jit(solution)/shard_map/all_to_all | solution.py:11
  38.2 15.3 %copy-start.6 = (bf16[1,128,2048]{2,1,0:T(8,128)(2,1)S(1)}, bf16[1,128,2048]{2,1,0:T(8,128)(2,1)}, u32[]{:S(2)}) copy-start(bf16[1,128,2048]{2,1,0:T(8,128)(2,1)} %param.16) | copy-start | bytes 1572868
  38.3 11.4 %copy-start.16 = (s32[256,1]{0,1:T(1,128)}, s32[256,1]{0,1:T(1,128)S(1)}, u32[]{:S(2)}) copy-start(s32[256,1]{0,1:T(1,128)S(1)} %compare_select_fusion.1) | copy-start | bytes 3076
  49.7 21.8 %all-to-all-start.3 = ((bf16[128,32,128]{2,0,1:T(8,128)(2,1)}), bf16[128,32,128]{2,0,1:T(8,128)(2,1)S(1)}, u32[]{:S(2)}, u32[]{:S(2)}) async-start(bf16[128,32,128]{2,0,1:T(8,128)(2,1)} %bitcast.18), calls=%async_computation.3 | async-start | bytes 2097152 | tf_op jit(solution)/shard_map/all_to_all | solution.py:158
  60.1 28.3 %copy-start.9 = (bf16[1,128,2048]{2,1,0:T(8,128)(2,1)S(1)}, bf16[1,128,2048]{2,1,0:T(8,128)(2,1)}, u32[]{:S(2)}) copy-start(bf16[1,128,2048]{2,1,0:T(8,128)(2,1)} %param.26) | copy-start | bytes 1572868
  71.5 109.1 %all-to-all-start = ((bf16[16,32,2048]{2,1,0:T(8,128)(2,1)}), bf16[16,32,2048]{2,1,0:T(8,128)(2,1)}, u32[]{:S(2)}, u32[]{:S(2)}) async-start(bf16[16,32,2048]{2,1,0:T(8,128)(2,1)} %broadcast_select_fusion), calls=%async_computation | async-start | bytes 4194304 | tf_op jit(solution)/shard_map/all_to_all | solution.py:104
  86.9 103.4 %all-gather.11.cloned.1.call-start = ((), (), s32[]{:S(2)}) async-start(), calls=%async_computation.11 | async-start | bytes 2162688 | tf_op jit(solution)/shard_map/all_gather | solution.py:115
  87.7 125.2 %all-gather.9.cloned.1.call-start = ((), (), s32[]{:S(2)}) async-start(), calls=%async_computation.10 | async-start | bytes 2162688 | tf_op jit(solution)/shard_map/all_gather | solution.py:111
  181.8 37.7 %all-to-all-start.7 = ((bf16[128,32,128]{2,0,1:T(8,128)(2,1)}), bf16[128,32,128]{2,0,1:T(8,128)(2,1)S(1)}, u32[]{:S(2)}, u32[]{:S(2)}) async-start(bf16[128,32,128]{2,0,1:T(8,128)(2,1)} %bitcast.66), calls=%async_computation.7 | async-start | bytes 2097152 | tf_op jit(solution)/shard_map/all_to_all | solution.py:157
  220.5 102.4 %all-to-all-start.1 = ((bf16[16,32,2048]{2,1,0:T(8,128)(2,1)}), bf16[16,32,2048]{2,1,0:T(8,128)(2,1)S(1)}, u32[]{:S(2)}, u32[]{:S(2)}) async-start(bf16[16,32,2048]{2,1,0:T(8,128)(2,1)} %bitcast.345), calls=%async_computation.1 | async-start | bytes 4194304 | tf_op jit(solution)/shard_map/all_to_all | solution.py:119
  322.9 24.2 %all-to-all-start.6 = ((bf16[128,32,128]{2,0,1:T(8,128)(2,1)}), bf16[128,32,128]{2,0,1:T(8,128)(2,1)}, u32[]{:S(2)}, u32[]{:S(2)}) async-start(bf16[128,32,128]{2,0,1:T(8,128)(2,1)} %copy.108), calls=%async_computation.6 | async-start | bytes 2097152 | tf_op jit(solution)/shard_map/all_to_all | solution.py:159
  335.1 6.7 copy-start.7
  335.1 16.0 %copy-start.12 = (f32[128,32]{0,1:T(8,128)S(1)}, f32[128,32]{0,1:T(8,128)}, u32[]{:S(2)}) copy-start(f32[128,32]{0,1:T(8,128)} %multiply_reduce_fusion) | copy-start | bytes 49156
  335.1 16.0 %copy-start.13 = (f32[32,128]{1,0:T(8,128)S(1)}, f32[32,128]{1,0:T(8,128)}, u32[]{:S(2)}) copy-start(f32[32,128]{1,0:T(8,128)} %multiply_bitcast_fusion.1) | copy-start | bytes 49156
  347.1 11.3 %all-to-all-start.2 = ((bf16[128,32,1]{0,2,1:T(2,128)(2,1)}), bf16[128,32,1]{0,2,1:T(2,128)(2,1)S(1)}, u32[]{:S(2)}, u32[]{:S(2)}) async-start(bf16[128,32,1]{0,2,1:T(2,128)(2,1)} %copy.101), calls=%async_computation.2 | async-start | bytes 32768 | tf_op jit(solution)/shard_map/all_to_all | solution.py:162
  355.0 20.3 %copy-start.3 = (bf16[64,64,64]{2,1,0:T(8,128)(2,1)S(1)}, bf16[64,64,64]{2,1,0:T(8,128)(2,1)}, u32[]{:S(2)}) copy-start(bf16[64,64,64]{2,1,0:T(8,128)(2,1)} %copy.109) | copy-start | bytes 1572868
  358.5 14.5 %all-to-all-start.5 = ((bf16[128,32,1]{0,2,1:T(2,128)(2,1)}), bf16[128,32,1]{0,2,1:T(2,128)(2,1)}, u32[]{:S(2)}, u32[]{:S(2)}) async-start(bf16[128,32,1]{0,2,1:T(2,128)(2,1)} %copy.105), calls=%async_computation.5 | async-start | bytes 32768 | tf_op jit(solution)/shard_map/all_to_all | solution.py:161
  381.4 3.7 copy-start.17
  385.1 339.8 %copy-start.11 = (f32[64,64]{1,0:T(8,128)S(1)}, f32[64,64]{1,0:T(8,128)}, u32[]{:S(2)}) copy-start(f32[64,64]{1,0:T(8,128)} %mul.296) | copy-start | bytes 49156
  385.1 339.8 %copy-start.14 = (pred[64,64]{1,0:T(8,128)(4,1)S(1)}, pred[64,64]{1,0:T(8,128)(4,1)}, u32[]{:S(2)}) copy-start(pred[64,64]{1,0:T(8,128)(4,1)} %iota_compare_fusion.2) | copy-start | bytes 12292
  (5 other events, 8.0 us)
Sparse Core Ops, SparseCore 0:
  11.2 68.2 all-gather.6
  90.9 57.2 all-gather.10
  151.3 61.4 all-gather.8
